TPU v7x, 32 devices: a whole 2x2x4 slice. The times are simulated.
32 devices in a mesh: dp: 4 (over x, core), fsdp: 8 (over z, y).
Axes of the slice: x: 2, y: 2, z: 4, core: 2. Of those that a mesh axis runs over, the one named last changes fastest.
Arguments:
- tokens: bfloat16 [8192, 2048], P(('dp', 'fsdp')), may hold values from -6 to 6
- w_q: bfloat16 [2048, 2048], P(('dp', 'fsdp')), may hold values from -0.125 to 0.125
- w_kv: bfloat16 [2048, 256], P(('dp', 'fsdp')), may hold values from -0.125 to 0.125
- g_attn: bfloat16 [2048], P(('dp', 'fsdp')), may hold values from 0.25 to 1.75
- g_mlp: bfloat16 [2048], P(('dp', 'fsdp')), may hold values from 0.25 to 1.75
- w_o: bfloat16 [2048, 2048], P(('dp', 'fsdp')), may hold values from -0.75 to 0.75
- w_gu: bfloat16 [5632, 2, 2048], P(('dp', 'fsdp')), may hold values from -0.125 to 0.125
- w_down: bfloat16 [5632, 2048], P(('dp', 'fsdp')), may hold values from -0.078125 to 0.078125
- grad_out: bfloat16 [8192, 2048], P(('dp', 'fsdp')), may hold values from -6 to 6
- grad_kv: bfloat16 [8192, 256], P(('dp', 'fsdp')), may hold values from -4 to 4
- group_id: int32 [32], P(('dp', 'fsdp')), may hold values from 0 to 7
- group_size: int32 [8], replicated, may hold values from 1 to 4
- group_weight: float32 [8], replicated, may hold values from 1 to 4
Outputs:
- output: bfloat16 [8192, 2048], P(('dp', 'fsdp'))
- d_tokens: float32 [8192, 2048], P(('dp', 'fsdp'))
- kv_out: bfloat16 [8192, 256], P(('dp', 'fsdp'))
- d_kv: float32 [8192, 256], P(('dp', 'fsdp'))
- d_w_q: float32 [2048, 2048], P(('dp', 'fsdp'))
- d_w_kv: float32 [2048, 256], P(('dp', 'fsdp'))
- d_g_attn: float32 [2048], P(('dp', 'fsdp'))
- d_g_mlp: float32 [2048], P(('dp', 'fsdp'))
- d_w_o: float32 [2048, 2048], P(('dp', 'fsdp'))
- d_w_gu: float32 [5632, 2, 2048], P(('dp', 'fsdp'))
- d_w_down: float32 [5632, 2048], P(('dp', 'fsdp'))
All inputs are finite; a program needn't handle non-finite values.
Results may differ from a plain program's by a relative error of at most 0.015.
Values may be sent and summed in bfloat16 or wider, within the bound.
No kernel may reach another device: no remote copies, remote signals or barrier semaphores. Data moves between devices by JAX's collectives and lax.ppermute only.
A program may use at most 256 MiB of HBM per device.

v0:
```python
import jax
import jax.numpy as jnp
from jax import lax
from jax.sharding import PartitionSpec as P

epsilon = 1e-05
theta_base = 10000.0


def rope_tables(length, width):
    halfway = width // 2
    freqs = theta_base ** (-(jnp.arange(halfway, dtype=jnp.float32) * 2.0 / width))
    angles = jnp.arange(length, dtype=jnp.float32)[:, None] * freqs[None, :]
    return (jnp.cos(angles), jnp.sin(angles))


def rotate(vectors, cosines, sine_part):
    halfway = vectors.shape[-1] // 2
    front = vectors[..., :halfway]
    behind = vectors[..., halfway:]
    return jnp.concatenate(
        [front * cosines - behind * sine_part, behind * cosines + front * sine_part], axis=-1
    )


def contract_last(left, right):
    return lax.dot_general(
        left,
        right,
        (((left.ndim - 1,), (right.ndim - 1,)), ((), ())),
        preferred_element_type=jnp.float32,
    )


def contract_first(left, right):
    return lax.dot_general(
        left, right, (((0,), (0,)), ((), ())), preferred_element_type=jnp.float32
    )


def local(
    tokens,
    w_q,
    w_kv,
    g_attn,
    g_mlp,
    w_o,
    w_gu,
    w_down,
    grad_out,
    grad_kv,
    group_id,
    group_size,
    group_weight,
):
    length, width = tokens.shape
    head_dim = grad_kv.shape[1] // 2
    q_width = w_q.shape[1]
    head_count = q_width // head_dim
    matches = jnp.arange(group_size.shape[0], dtype=jnp.int32) == group_id[0]
    factor = jnp.sum(jnp.where(matches, group_weight / group_size.astype(jnp.float32), 0.0))
    cosines, sine_part = rope_tables(length, head_dim)
    x_full = tokens.astype(jnp.float32)
    inv_one = lax.rsqrt(jnp.mean(x_full * x_full, axis=-1, keepdims=True) + epsilon)
    normed_one = x_full * inv_one
    wq_piece = lax.all_gather(w_q, ("dp", "fsdp"), axis=0, tiled=True)
    wkv_piece = lax.all_gather(w_kv, ("dp", "fsdp"), axis=0, tiled=True)
    gain_piece = lax.all_gather(g_attn, ("dp", "fsdp"), axis=0, tiled=True)
    mlp_gain_piece = lax.all_gather(g_mlp, ("dp", "fsdp"), axis=0, tiled=True)
    normed_cols = normed_one
    h_cols = (normed_cols * gain_piece.astype(jnp.float32)).astype(jnp.bfloat16)
    q_acc = jnp.dot(h_cols, wq_piece, preferred_element_type=jnp.float32)
    kv_acc = jnp.dot(h_cols, wkv_piece, preferred_element_type=jnp.float32)
    gain_two = mlp_gain_piece.astype(jnp.float32)
    q_pre, kv_pre, gain_two, h_one = (q_acc, kv_acc, gain_two, h_cols)
    q_low = rotate(
        q_pre.reshape(length, head_count, head_dim), cosines[:, None, :], sine_part[:, None, :]
    ).astype(jnp.bfloat16)
    k_low = rotate(kv_pre[:, :head_dim], cosines, sine_part).astype(jnp.bfloat16)
    v_low = kv_pre[:, head_dim:].astype(jnp.bfloat16)
    score_scale = head_dim ** (-0.5)
    causal = jnp.arange(length)[:, None] >= jnp.arange(length)[None, :]

    def logits_of(queries, keys):
        raw_scores = jnp.einsum("thd,sd->hts", queries, keys, preferred_element_type=jnp.float32)
        return jnp.where(causal[None], raw_scores * score_scale, -1e30)

    logits = logits_of(q_low, k_low)
    row_top = jnp.max(logits, axis=-1, keepdims=True)
    exp_vals = jnp.exp(logits - row_top)
    row_total = jnp.sum(exp_vals, axis=-1, keepdims=True)
    prob_full = exp_vals / row_total
    log_total = row_top + jnp.log(row_total)
    prob_low = prob_full.astype(jnp.bfloat16)
    attended = jnp.einsum("hts,sd->thd", prob_low, v_low, preferred_element_type=jnp.float32)
    attn_low = attended.reshape(length, q_width).astype(jnp.bfloat16)
    branch = jnp.dot(
        attn_low,
        lax.all_gather(w_o, ("dp", "fsdp"), axis=0, tiled=True),
        preferred_element_type=jnp.float32,
    )
    x_mid = x_full + branch
    inv_two = lax.rsqrt(jnp.mean(x_mid * x_mid, axis=-1, keepdims=True) + epsilon)
    normed_two = x_mid * inv_two
    h_two = (normed_two * gain_two).astype(jnp.bfloat16)
    grad_top = grad_out.astype(jnp.float32) * factor
    grad_low = grad_top.astype(jnp.bfloat16)
    ff_rows, grad_rows = (
        lax.all_gather(h_two, "dp", axis=0, tiled=True),
        lax.all_gather(grad_low, "dp", axis=0, tiled=True),
    )
    gu_piece = lax.all_gather(w_gu, "fsdp", axis=0, tiled=True)
    down_piece = lax.all_gather(w_down, "fsdp", axis=0, tiled=True)
    both_proj = jnp.einsum("td,fkd->tkf", ff_rows, gu_piece, preferred_element_type=jnp.float32)
    gate_vals = both_proj[:, 0]
    up_vals = both_proj[:, 1]
    hid_cols = (jax.nn.silu(gate_vals) * up_vals).astype(jnp.bfloat16)
    mlp_out = jnp.dot(hid_cols, down_piece, preferred_element_type=jnp.float32)
    mlp_part = mlp_out
    gate_all = gate_vals
    up_all = up_vals
    mlp_out = lax.psum_scatter(
        mlp_part.astype(jnp.bfloat16), "dp", scatter_dimension=0, tiled=True
    ).astype(jnp.float32)
    gu_piece = lax.all_gather(w_gu, "fsdp", axis=0, tiled=True)
    down_piece = lax.all_gather(w_down, "fsdp", axis=0, tiled=True)
    gate_vals = gate_all
    up_vals = up_all
    d_hid = contract_last(grad_rows, down_piece)
    sigmoid_vals = jax.nn.sigmoid(gate_vals)
    d_gate = d_hid * up_vals * sigmoid_vals * (1.0 + gate_vals * (1.0 - sigmoid_vals))
    d_up = d_hid * gate_vals * sigmoid_vals
    d_both = jnp.stack([d_gate, d_up], axis=1).astype(jnp.bfloat16)
    d_h_two = jnp.einsum("tkf,fkd->td", d_both, gu_piece, preferred_element_type=jnp.float32)
    d_h_part = d_h_two
    d_h_two = lax.psum_scatter(
        d_h_part.astype(jnp.bfloat16), "dp", scatter_dimension=0, tiled=True
    ).astype(jnp.float32)
    d_w_down = lax.psum_scatter(
        contract_first(hid_cols, grad_rows).astype(jnp.bfloat16),
        "fsdp",
        scatter_dimension=0,
        tiled=True,
    ).astype(jnp.float32)
    d_w_gu = lax.psum_scatter(
        jnp.einsum("tkf,td->fkd", d_both, ff_rows, preferred_element_type=jnp.float32).astype(
            jnp.bfloat16
        ),
        "fsdp",
        scatter_dimension=0,
        tiled=True,
    ).astype(jnp.float32)
    output = (x_mid + mlp_out).astype(jnp.bfloat16)
    d_gain_two = jnp.sum(d_h_two * normed_two, axis=0)
    d_normed_two = d_h_two * gain_two
    d_mid = grad_top + inv_two * (
        d_normed_two - normed_two * jnp.mean(d_normed_two * normed_two, axis=-1, keepdims=True)
    )
    d_mid_low = d_mid.astype(jnp.bfloat16)
    d_attended = contract_last(d_mid_low, lax.all_gather(w_o, ("dp", "fsdp"), axis=0, tiled=True))
    d_att_low = d_attended.astype(jnp.bfloat16).reshape(length, head_count, head_dim)
    d_w_o = lax.psum_scatter(
        contract_first(attn_low, d_mid_low), ("dp", "fsdp"), scatter_dimension=0, tiled=True
    )
    prob_back = jnp.exp(logits_of(q_low, k_low) - log_total)
    prob_back_low = prob_back.astype(jnp.bfloat16)
    d_probs = jnp.einsum("thd,sd->hts", d_att_low, v_low, preferred_element_type=jnp.float32)
    d_v_own = jnp.einsum(
        "hts,thd->sd", prob_back_low, d_att_low, preferred_element_type=jnp.float32
    )
    d_logit = prob_back * (d_probs - jnp.sum(prob_back * d_probs, axis=-1, keepdims=True))
    d_raw = (d_logit * score_scale).astype(jnp.bfloat16)
    d_q_rot = jnp.einsum("hts,sd->thd", d_raw, k_low, preferred_element_type=jnp.float32)
    d_k_own = jnp.einsum("hts,thd->sd", d_raw, q_low, preferred_element_type=jnp.float32)
    kv_extra = grad_kv.astype(jnp.float32) * factor
    d_k_total = d_k_own + kv_extra[:, :head_dim]
    d_v_total = d_v_own + kv_extra[:, head_dim:]
    d_kv = jnp.concatenate([d_k_total, d_v_total], axis=1)
    d_kv_low = jnp.concatenate([rotate(d_k_total, cosines, -sine_part), d_v_total], axis=1).astype(
        jnp.bfloat16
    )
    d_q_low = (
        rotate(d_q_rot, cosines[:, None, :], -sine_part[:, None, :])
        .reshape(length, q_width)
        .astype(jnp.bfloat16)
    )
    wq_piece = lax.all_gather(w_q, ("dp", "fsdp"), axis=0, tiled=True)
    wkv_piece = lax.all_gather(w_kv, ("dp", "fsdp"), axis=0, tiled=True)
    gain_piece = lax.all_gather(g_attn, ("dp", "fsdp"), axis=0, tiled=True)
    d_h_cols = contract_last(d_q_low, wq_piece) + contract_last(d_kv_low, wkv_piece)
    normed_cols = normed_one
    d_normed = d_h_cols * gain_piece.astype(jnp.float32)
    d_gain = jnp.sum(d_h_cols * normed_cols, axis=0)
    d_tokens = d_mid + inv_one * (
        d_normed - normed_one * jnp.mean(d_normed * normed_one, axis=-1, keepdims=True)
    )
    joined = jnp.concatenate([d_q_low, d_kv_low], axis=1)
    d_w_in = lax.psum_scatter(
        contract_first(h_one, joined), ("dp", "fsdp"), scatter_dimension=0, tiled=True
    )
    d_g_attn, d_g_mlp = (
        lax.psum_scatter(d_gain, ("dp", "fsdp"), scatter_dimension=0, tiled=True),
        lax.psum_scatter(d_gain_two, ("dp", "fsdp"), scatter_dimension=0, tiled=True),
    )
    kv_out = jnp.concatenate([k_low, v_low], axis=1)
    return (
        output,
        d_tokens,
        kv_out,
        d_kv,
        d_w_in[:, :q_width],
        d_w_in[:, q_width:],
        d_g_attn,
        d_g_mlp,
        d_w_o,
        d_w_gu,
        d_w_down,
    )


def solution(mesh):
    placed = (
        P(("dp", "fsdp"), None),
        P(("dp", "fsdp"), None),
        P(("dp", "fsdp"), None),
        P(("dp", "fsdp")),
        P(("dp", "fsdp")),
        P(("dp", "fsdp"), None),
        P(("dp", "fsdp"), None, None),
        P(("dp", "fsdp"), None),
        P(("dp", "fsdp"), None),
        P(("dp", "fsdp"), None),
        P(("dp", "fsdp")),
        P(),
        P(),
    )
    return jax.shard_map(
        local,
        mesh=mesh,
        in_specs=placed,
        out_specs=(
            P(("dp", "fsdp"), None),
            P(("dp", "fsdp"), None),
            P(("dp", "fsdp"), None),
            P(("dp", "fsdp"), None),
            P(("dp", "fsdp"), None),
            P(("dp", "fsdp"), None),
            P(("dp", "fsdp")),
            P(("dp", "fsdp")),
            P(("dp", "fsdp"), None),
            P(("dp", "fsdp"), None, None),
            P(("dp", "fsdp"), None),
        ),
        check_vma=False,
    )
```

profile of v0, /device:TPU:0, one launch (start us, length us, event | category | flops | bytes accessed | tf_op | source)
XLA Modules:
  0.0 1734.8 jit_solution(2765132462502652689)
XLA Ops:
  9.5 3.0 copy.76
  13.1 42.2 %all-reduce.6 = (bf16[2048]{0:T(1024)(128)(2,1)S(1)}, bf16[2048]{0:T(1024)(128)(2,1)S(1)}) all-reduce(bf16[2048]{0:T(1024)(128)(2,1)S(1)} %dynamic-update-slice, bf16[2048]{0:T(1024)(128)(2,1)S(1)} %dynamic-update-slice.1), channel_id=1, replica_groups=mesh['dp'=4,'fsdp'=8] {'dp','fsdp'}, use_global_device_ids=true, to_apply=%add | all-reduce | flops 4096 | bytes 16384
  55.6 12.1 all-gather.8.cloned.1.call-done
  67.8 1.9 fusion.81
  70.2 76.8 %all-gather.10.cloned.1.call-done = bf16[2048,2048]{1,0:T(8,128)(2,1)} async-done(((bf16[64,2048]{1,0:T(8,128)(2,1)}), bf16[2048,2048]{1,0:T(8,128)(2,1)}) %all-gather.10.cloned.1.call-update) | async-done | bytes 8388624 | tf_op jit(solution)/shard_map/all_gather | solution.py:66
  147.0 5.8 convolution_bitcast_fusion.1
  158.7 2.0 fusion.36
  160.6 65.3 %all-gather.12.cloned.1.call-done = bf16[2048,2048]{1,0:T(8,128)(2,1)} async-done(((bf16[64,2048]{1,0:T(8,128)(2,1)}), bf16[2048,2048]{1,0:T(8,128)(2,1)}) %all-gather.12.cloned.1.call-update) | async-done | bytes 8388624 | tf_op jit(solution)/shard_map/all_gather | solution.py:99
  225.9 6.2 multiply_reduce_fusion
  234.7 3.2 fusion.33
  239.1 151.7 %all-gather.16.cloned.1.call-done = bf16[1408,2,2048]{2,0,1:T(8,128)(2,1)} async-done(((bf16[176,2,2048]{2,0,1:T(8,128)(2,1)}), bf16[1408,2,2048]{2,0,1:T(8,128)(2,1)}) %all-gather.16.cloned.1.call-update) | async-done | bytes 11534352 | tf_op jit(solution)/shard_map/all_gather | solution.py:112
  390.8 34.7 %all-gather.14.cloned.1.call-done = bf16[1024,2048]{1,0:T(8,128)(2,1)} async-done(((bf16[256,2048]{1,0:T(8,128)(2,1)}), bf16[1024,2048]{1,0:T(8,128)(2,1)}) %all-gather.14.cloned.1.call-update) | async-done | bytes 4194320 | tf_op jit(solution)/shard_map/all_gather | solution.py:109
  425.5 18.8 %convolution_bitcast_fusion = f32[1024,2,1408]{2,0,1:T(8,128)} fusion(bf16[1408,2,2048]{2,0,1:T(8,128)(2,1)} %all-gather.16.cloned.1.call-done, bf16[1024,2048]{1,0:T(8,128)(2,1)} %all-gather.14.cloned.1.call-done), kind=kOutput, calls=%fused_computation.4 | convolution fusion | flops 11811160064 | bytes 27262976 | tf_op jit(solution)/shard_map/td,fkd->tkf/dot_general | solution.py:114
  444.3 17.7 %all-gather.20.cloned.1.call-done = bf16[1024,2048]{1,0:T(8,128)(2,1)} async-done(((bf16[256,2048]{1,0:T(8,128)(2,1)}), bf16[1024,2048]{1,0:T(8,128)(2,1)}) %all-gather.20.cloned.1.call-update) | async-done | bytes 4194320 | tf_op jit(solution)/shard_map/all_gather | solution.py:110
  462.0 94.9 %all-gather.18.cloned.1.call-done = bf16[1408,2048]{1,0:T(8,128)(2,1)} async-done(((bf16[176,2048]{1,0:T(8,128)(2,1)}), bf16[1408,2048]{1,0:T(8,128)(2,1)}) %all-gather.18.cloned.1.call-update) | async-done | bytes 5767184 | tf_op jit(solution)/shard_map/all_gather | solution.py:113
  556.9 15.6 fusion.13
  572.5 1.6 copy-done.30
  575.0 16.3 bitcast_convert_fusion
  591.6 10.9 convolution_convert_fusion.1
  602.6 10.5 convolution_convert_fusion
  613.2 18.3 %convert_bitcast_fusion = bf16[1408,2,2048]{0,2,1:T(8,128)(2,1)} fusion(bf16[1024,2048]{1,0:T(8,128)(2,1)} %all-gather.14.cloned.1.call-done, bf16[1024,1,1408]{2,0,1:T(8,128)(2,1)} %copy-done.31, bf16[1024,1,1408]{2,0,1:T(8,128)(2,1)} %copy-done.30), kind=kOutput, calls=%fused_computation.1 | convolution fusion | flops 11828461568 | bytes 21495808 | tf_op jit(solution)/shard_map/tkf,td->fkd/dot_general | solution.py:146
  631.6 29.4 %copy.89 = bf16[1408,2,2048]{2,1,0:T(2,128)(2,1)} copy(bf16[1408,2,2048]{0,2,1:T(8,128)(2,1)} %convert_bitcast_fusion) | data formatting | bytes 23068672 | tf_op jit(solution)/shard_map/convert_element_type | solution.py:146
  662.6 1.6 convert_multiply_fusion.5
  664.2 1.4 log_add_fusion
  665.6 2.6 fusion.19
  668.8 12.7 reduce-scatter.6.cloned.1.call-done
  681.5 4.4 fusion.18
  687.3 5.7 convolution_convert_fusion.2
  693.6 3.7 fusion.61
  697.2 9.2 fusion.49
  707.8 9.5 fusion.35
  717.3 3.2 subtract_convert_fusion
  720.4 1.6 pad_maximum_fusion.4
  722.0 1.5 copy.82
  723.5 4.1 fusion.85
  727.6 8.2 fusion.37
  737.4 9.3 fusion.53
  752.2 6.2 fusion.88
  758.4 2.3 fusion.25
  760.6 42.5 %all-reduce.5 = (f32[2048]{0:T(1024)S(1)}, f32[2048]{0:T(1024)S(1)}) all-reduce(f32[2048]{0:T(1024)S(1)} %get-tuple-element.46, f32[2048]{0:T(1024)S(1)} %copy-done.21), channel_id=5, replica_groups=mesh['dp'=4,'fsdp'=8] {'dp','fsdp'}, use_global_device_ids=true, to_apply=%region_12.13.clone | all-reduce | flops 4096 | bytes 32768
  804.3 4.1 fusion.24
  808.4 2.4 convert_element_type.122
  810.8 345.1 %all-reduce.9.cloned.1.call-done = bf16[1408,2,2048]{2,1,0:T(2,128)(2,1)} async-done(((bf16[1408,2,2048]{2,1,0:T(2,128)(2,1)}), bf16[1408,2,2048]{2,1,0:T(2,128)(2,1)}) %all-reduce.9.cloned.1.call-update) | async-done | bytes 11534352
  1155.9 4.6 dynamic-slice_convert_fusion
  1160.5 207.4 %reduce-scatter.10.cloned.1.call-done = f32[64,2304]{1,0:T(8,128)} async-done(((f32[2048,2304]{1,0:T(8,128)}), f32[64,2304]{1,0:T(8,128)}) %reduce-scatter.10.cloned.1.call-update) | async-done | bytes 589840 | tf_op jit(solution)/shard_map/reduce_scatter | solution.py:198
  1367.9 1.9 slice.77
  1369.8 1.5 slice.78
  1371.3 356.5 %reduce-scatter.12.cloned.1.call-done = f32[64,2048]{1,0:T(8,128)} async-done(((f32[2048,2048]{1,0:T(8,128)}), f32[64,2048]{1,0:T(8,128)}) %reduce-scatter.12.cloned.1.call-update) | async-done | bytes 524304 | tf_op jit(solution)/shard_map/reduce_scatter | solution.py:162
  (126 shorter events, 26.6 us)
Async XLA Ops:
  7.2 5.4 copy-start.27
  7.2 5.7 copy-start.28
  7.2 48.1 %copy-start.1 = (bf16[256,2048]{1,0:T(8,128)(2,1)S(1)}, bf16[256,2048]{1,0:T(8,128)(2,1)}, u32[]{:S(2)}) copy-start(bf16[256,2048]{1,0:T(8,128)(2,1)} %param.13) | copy-start | bytes 3145732
  7.2 60.6 %all-gather.8.cloned.1.call-start = ((), (), s32[]{:S(2)}) async-start(), calls=%async_computation.5 | async-start | bytes 1081344 | tf_op jit(solution)/shard_map/all_gather | solution.py:67
  7.9 139.1 %all-gather.10.cloned.1.call-start = ((), (), s32[]{:S(2)}) async-start(), calls=%async_computation.6 | async-start | bytes 8650752 | tf_op jit(solution)/shard_map/all_gather | solution.py:66
  8.7 217.2 %all-gather.12.cloned.1.call-start = ((), (), s32[]{:S(2)}) async-start(), calls=%async_computation.7 | async-start | bytes 8650752 | tf_op jit(solution)/shard_map/all_gather | solution.py:99
  9.4 381.4 %all-gather.16.cloned.1.call-start = ((), (), s32[]{:S(2)}) async-start(), calls=%async_computation.9 | async-start | bytes 12976128 | tf_op jit(solution)/shard_map/all_gather | solution.py:112
  12.5 413.0 %all-gather.14.cloned.1.call-start = ((), (), s32[]{:S(2)}) async-start(), calls=%async_computation.8 | async-start | bytes 5242880 | tf_op jit(solution)/shard_map/all_gather | solution.py:109
  55.3 14.7 copy-start.23
  55.6 97.2 %copy-start.19 = (f32[256]{0:T(256)}, f32[256]{0:T(256)S(1)}, u32[]{:S(2)}) copy-start(f32[256]{0:T(256)S(1)} %add_rsqrt_fusion.1) | copy-start | bytes 3076
  69.6 87.6 %copy-start.11 = (f32[256,256]{0,1:T(8,128)}, f32[256,256]{0,1:T(8,128)S(1)}, u32[]{:S(2)}) copy-start(f32[256,256]{0,1:T(8,128)S(1)} %fusion.81) | copy-start | bytes 786436
  70.0 85.3 %copy-start.12 = (bf16[256,64]{0,1:T(8,128)(2,1)}, bf16[256,64]{0,1:T(8,128)(2,1)S(1)}, u32[]{:S(2)}) copy-start(bf16[256,64]{0,1:T(8,128)(2,1)S(1)} %get-tuple-element.63) | copy-start | bytes 98308
  70.0 85.3 %copy-start.14 = (bf16[256,64]{0,1:T(8,128)(2,1)}, bf16[256,64]{0,1:T(8,128)(2,1)S(1)}, u32[]{:S(2)}) copy-start(bf16[256,64]{0,1:T(8,128)(2,1)S(1)} %get-tuple-element.64) | copy-start | bytes 98308
  155.2 1.4 copy-start.4
  155.2 1.4 copy-start.6
  156.7 2.0 copy-start
  156.7 4.0 copy-start.16
  158.7 2.0 copy-start.18
  232.1 2.0 copy-start.25
  232.1 2.0 copy-start.26
  232.1 5.8 copy-start.22
  233.4 228.6 %all-gather.20.cloned.1.call-start = ((), (), s32[]{:S(2)}) async-start(), calls=%async_computation.12 | async-start | bytes 5242880 | tf_op jit(solution)/shard_map/all_gather | solution.py:110
  237.9 318.9 %all-gather.18.cloned.1.call-start = ((), (), s32[]{:S(2)}) async-start(), calls=%async_computation.10 | async-start | bytes 6488064 | tf_op jit(solution)/shard_map/all_gather | solution.py:113
  238.7 427.0 %reduce-scatter.8.cloned.1.call-start = ((), (), s32[]{:S(2)}) async-start(), calls=%async_computation.13 | async-start | bytes 5242880 | tf_op jit(solution)/shard_map/reduce_scatter | solution.py:136
  572.5 1.6 copy-start.30
  572.5 2.5 copy-start.31
  591.4 90.1 %reduce-scatter.6.cloned.1.call-start = ((), (), s32[]{:S(2)}) async-start(), calls=%async_computation.11 | async-start | bytes 5242880 | tf_op jit(solution)/shard_map/reduce_scatter | solution.py:122
  602.6 205.8 %reduce-scatter.14.cloned.1.call-start = ((), (), s32[]{:S(2)}) async-start(), calls=%async_computation.16 | async-start | bytes 6488064 | tf_op jit(solution)/shard_map/reduce_scatter | solution.py:139
  613.2 542.7 %all-reduce.9.cloned.1.call-start = ((), (), s32[]{:S(2)}) async-start(), calls=%async_computation.17 | async-start | bytes 23068672
  661.0 0.9 copy-start.17
  661.0 706.9 %reduce-scatter.10.cloned.1.call-start = ((), (), s32[]{:S(2)}) async-start(), calls=%async_computation.14 | async-start | bytes 19464192 | tf_op jit(solution)/shard_map/reduce_scatter | solution.py:198
  664.2 33.0 %copy-start.9 = (f32[256,256]{0,1:T(8,128)}, f32[256,256]{0,1:T(8,128)S(1)}, u32[]{:S(2)}) copy-start(f32[256,256]{0,1:T(8,128)S(1)} %convert_multiply_fusion.5) | copy-start | bytes 786436
  685.9 1.3 copy-start.2
  693.5 3.7 copy-start.5
  697.2 9.3 copy-start.24
  720.4 3.1 copy-start.10
  723.5 12.3 copy-start.7
  723.5 4.1 copy-start.20
  735.8 1.6 copy-start.3
  735.8 992.0 %reduce-scatter.12.cloned.1.call-start = ((), (), s32[]{:S(2)}) async-start(), calls=%async_computation.15 | async-start | bytes 17301504 | tf_op jit(solution)/shard_map/reduce_scatter | solution.py:162
  746.7 0.7 copy-start.29
  746.7 2.8 copy-start.13
  746.7 2.8 copy-start.15
  752.2 6.2 copy-start.8
  758.4 2.3 copy-start.21
Sparse Core Ops, SparseCore 0:
  11.1 56.5 all-gather.7
  70.7 76.2 all-gather.9
  150.0 75.8 all-gather.11
  228.5 162.2 all-gather.15
  392.8 32.6 all-gather.13
  427.5 34.4 all-gather.19
  464.2 92.6 all-gather.17
  591.5 42.6 reduce-scatter.7
  636.9 44.5 reduce-scatter.5
  685.0 111.5 reduce-scatter.13
  800.5 355.3 all-reduce.8
  1162.1 205.7 reduce-scatter.9
  1370.8 356.9 reduce-scatter.11
where the time goes:
time: 1750 us; the launch traced here: 1730 us
  waiting for transfers between devices  1380 us (79%)
  matrix products  166 us (9%)
  blocking collectives  84.7 us (5%)
  local copies, waits for them, and re-layouts  52.5 us (3%)
  other arithmetic  36.2 us (2%)
    reduce_scatter x1, waiting for transfers between devices, local(): lax.psum_scatter(contract_first(attn_low, d_mid_low), ('dp', 'fsdp'), sca...  357 us
    unnamed x14, waiting for transfers between devices  348 us
    reduce_scatter x1, waiting for transfers between devices, local(): lax.psum_scatter(contract_first(h_one, joined), ('dp', 'fsdp'), scatter_d...  207 us
    all_gather x1, waiting for transfers between devices, local(): gu_piece = lax.all_gather(w_gu, 'fsdp', axis=0, tiled=True)  152 us
    all_gather x1, waiting for transfers between devices, local(): down_piece = lax.all_gather(w_down, 'fsdp', axis=0, tiled=True)  94.9 us
    unnamed x2, blocking collectives  84.7 us
    all_gather x1, waiting for transfers between devices, local(): wq_piece = lax.all_gather(w_q, ('dp', 'fsdp'), axis=0, tiled=True)  76.8 us
    all_gather x1, waiting for transfers between devices, local(): lax.all_gather(w_o, ('dp', 'fsdp'), axis=0, tiled=True)  65.3 us
  transfers between devices with their start and end apart: 13, of which 11 were waited for; matrix products, arithmetic and copies ran while one was open for 12% of the time, Pallas kernels for 0%

commit v1 on v0

--- a/solution.py
+++ b/solution.py
@@ -63,8 +63,11 @@
     x_full = tokens.astype(jnp.float32)
     inv_one = lax.rsqrt(jnp.mean(x_full * x_full, axis=-1, keepdims=True) + epsilon)
     normed_one = x_full * inv_one
-    wq_piece = lax.all_gather(w_q, ("dp", "fsdp"), axis=0, tiled=True)
-    wkv_piece = lax.all_gather(w_kv, ("dp", "fsdp"), axis=0, tiled=True)
+    wq_piece, wkv_piece = jnp.split(
+        lax.all_gather(jnp.concatenate([w_q, w_kv], axis=1), ("dp", "fsdp"), axis=0, tiled=True),
+        [w_q.shape[1]],
+        axis=1,
+    )
     gain_piece = lax.all_gather(g_attn, ("dp", "fsdp"), axis=0, tiled=True)
     mlp_gain_piece = lax.all_gather(g_mlp, ("dp", "fsdp"), axis=0, tiled=True)
     normed_cols = normed_one

time: 1750 us -> 1830 us (1.046)
  waiting for transfers between devices: 1380 us -> 1460 us
    all_gather x1, waiting for transfers between devices: 76.8 us -> 9.1 us  [local(): wq_piece = lax.all_gather(w_q, ('dp', 'fsdp'), axis=0, tiled=True)]
    reduce_scatter x1, waiting for transfers between devices: 0.01 us -> 63.1 us  [local(): lax.psum_scatter(contract_first(hid_cols, grad_rows).astype(jnp.bfloat16)...]
    all_gather x0 -> x1, waiting for transfers between devices: none -> 40.3 us  [local(): lax.all_gather(jnp.concatenate([w_q, w_kv], axis=1), ('dp', 'fsdp'), axis...]
    all_gather x1, waiting for transfers between devices: 12.1 us -> 47.9 us  [local(): wkv_piece = lax.all_gather(w_kv, ('dp', 'fsdp'), axis=0, tiled=True)]
    unnamed x14 -> x15, waiting for transfers between devices: 348 us -> 360 us
  transfers between devices with their start and end apart: 13 -> 14, of which waited for: 11 -> 13; matrix products, arithmetic and copies ran while one was open for 12% -> 12% of each run, Pallas kernels for 0% -> 0%
where the time goes in v1:
time: 1830 us; the launch traced here: 1820 us
  waiting for transfers between devices  1460 us (80%)
  matrix products  170 us (9%)
  blocking collectives  84.2 us (5%)
  local copies, waits for them, and re-layouts  53.5 us (3%)
  other arithmetic  37.9 us (2%)
    unnamed x15, waiting for transfers between devices  360 us
    reduce_scatter x1, waiting for transfers between devices, local(): lax.psum_scatter(contract_first(attn_low, d_mid_low), ('dp', 'fsdp'), sca...  356 us
    reduce_scatter x1, waiting for transfers between devices, local(): lax.psum_scatter(contract_first(h_one, joined), ('dp', 'fsdp'), scatter_d...  208 us
    all_gather x1, waiting for transfers between devices, local(): gu_piece = lax.all_gather(w_gu, 'fsdp', axis=0, tiled=True)  152 us
    all_gather x1, waiting for transfers between devices, local(): down_piece = lax.all_gather(w_down, 'fsdp', axis=0, tiled=True)  94.7 us
    unnamed x2, blocking collectives  84.2 us
    reduce_scatter x1, waiting for transfers between devices, local(): lax.psum_scatter(contract_first(hid_cols, grad_rows).astype(jnp.bfloat16)...  63.1 us
    all_gather x1, waiting for transfers between devices, local(): lax.all_gather(w_o, ('dp', 'fsdp'), axis=0, tiled=True)  61.5 us
  transfers between devices with their start and end apart: 14, of which 13 were waited for; matrix products, arithmetic and copies ran while one was open for 12% of the time, Pallas kernels for 0%

profile of v1, /device:TPU:0, one launch (start us, length us, event | category | flops | bytes accessed | tf_op | source)
XLA Modules:
  0.0 1819.2 jit_solution(16553935627851297786)
XLA Ops:
  7.3 1.8 pad_maximum_fusion.5
  9.9 3.0 copy.76
  13.5 42.5 %all-reduce.6 = (bf16[2048]{0:T(1024)(128)(2,1)S(1)}, bf16[2048]{0:T(1024)(128)(2,1)S(1)}) all-reduce(bf16[2048]{0:T(1024)(128)(2,1)S(1)} %dynamic-update-slice, bf16[2048]{0:T(1024)(128)(2,1)S(1)} %dynamic-update-slice.1), channel_id=1, replica_groups=mesh['dp'=4,'fsdp'=8] {'dp','fsdp'}, use_global_device_ids=true, to_apply=%add | all-reduce | flops 4096 | bytes 16384
  56.4 40.3 %all-gather.9.cloned.1.call-done = bf16[2048,2304]{1,0:T(8,128)(2,1)} async-done(((bf16[64,2304]{1,0:T(8,128)(2,1)}), bf16[2048,2304]{1,0:T(8,128)(2,1)}) %all-gather.9.cloned.1.call-update) | async-done | bytes 9437200 | tf_op jit(solution)/shard_map/all_gather | solution.py:67
  96.6 5.7 fusion.38
  102.8 1.9 fusion.58
  112.3 1.9 fusion.41
  114.2 61.5 %all-gather.11.cloned.1.call-done = bf16[2048,2048]{1,0:T(8,128)(2,1)} async-done(((bf16[64,2048]{1,0:T(8,128)(2,1)}), bf16[2048,2048]{1,0:T(8,128)(2,1)}) %all-gather.11.cloned.1.call-update) | async-done | bytes 8388624 | tf_op jit(solution)/shard_map/all_gather | solution.py:102
  175.7 6.2 multiply_reduce_fusion
  184.4 3.2 fusion.35
  188.7 152.1 %all-gather.15.cloned.1.call-done = bf16[1408,2,2048]{2,0,1:T(8,128)(2,1)} async-done(((bf16[176,2,2048]{2,0,1:T(8,128)(2,1)}), bf16[1408,2,2048]{2,0,1:T(8,128)(2,1)}) %all-gather.15.cloned.1.call-update) | async-done | bytes 11534352 | tf_op jit(solution)/shard_map/all_gather | solution.py:115
  340.7 34.7 %all-gather.13.cloned.1.call-done = bf16[1024,2048]{1,0:T(8,128)(2,1)} async-done(((bf16[256,2048]{1,0:T(8,128)(2,1)}), bf16[1024,2048]{1,0:T(8,128)(2,1)}) %all-gather.13.cloned.1.call-update) | async-done | bytes 4194320 | tf_op jit(solution)/shard_map/all_gather | solution.py:112
  375.4 18.8 %convolution_bitcast_fusion = f32[1024,2,1408]{2,0,1:T(8,128)} fusion(bf16[1408,2,2048]{2,0,1:T(8,128)(2,1)} %all-gather.15.cloned.1.call-done, bf16[1024,2048]{1,0:T(8,128)(2,1)} %all-gather.13.cloned.1.call-done), kind=kOutput, calls=%fused_computation.6 | convolution fusion | flops 11811160064 | bytes 27262976 | tf_op jit(solution)/shard_map/td,fkd->tkf/dot_general | solution.py:117
  394.2 17.7 all-gather.19.cloned.1.call-done
  411.9 94.7 %all-gather.17.cloned.1.call-done = bf16[1408,2048]{1,0:T(8,128)(2,1)} async-done(((bf16[176,2048]{1,0:T(8,128)(2,1)}), bf16[1408,2048]{1,0:T(8,128)(2,1)}) %all-gather.17.cloned.1.call-update) | async-done | bytes 5767184 | tf_op jit(solution)/shard_map/all_gather | solution.py:116
  506.6 15.6 fusion.15
  522.3 1.6 copy-done.30
  524.8 16.3 bitcast_convert_fusion
  541.4 10.9 convolution_convert_fusion.1
  553.7 10.5 convolution_convert_fusion
  564.2 18.4 %convert_bitcast_fusion = bf16[1408,2,2048]{0,2,1:T(8,128)(2,1)} fusion(bf16[1024,2048]{1,0:T(8,128)(2,1)} %all-gather.13.cloned.1.call-done, bf16[1024,1,1408]{2,0,1:T(8,128)(2,1)} %copy-done.31, bf16[1024,1,1408]{2,0,1:T(8,128)(2,1)} %copy-done.30), kind=kOutput, calls=%fused_computation.1 | convolution fusion | flops 11828461568 | bytes 21495808 | tf_op jit(solution)/shard_map/tkf,td->fkd/dot_general | solution.py:149
  582.6 29.4 %copy.89 = bf16[1408,2,2048]{2,1,0:T(2,128)(2,1)} copy(bf16[1408,2,2048]{0,2,1:T(8,128)(2,1)} %convert_bitcast_fusion) | data formatting | bytes 23068672 | tf_op jit(solution)/shard_map/convert_element_type | solution.py:149
  613.7 1.6 convert_multiply_fusion.5
  616.7 2.6 fusion.21
  619.9 11.3 reduce-scatter.6.cloned.1.call-done
  631.2 4.4 fusion.20
  637.0 5.7 convolution_convert_fusion.2
  643.3 3.7 fusion.68
  647.0 9.3 fusion.54
  657.6 9.6 fusion.37
  667.2 3.0 subtract_convert_fusion
  670.3 1.6 pad_maximum_fusion.4
  673.3 4.1 fusion.91
  677.4 8.7 fusion.42
  687.8 9.3 fusion.60
  702.5 9.1 all-gather.21.cloned.1.call-done
  711.6 7.4 fusion.94
  719.1 47.9 %all-gather.23.cloned.1.call-done = bf16[2048,256]{1,0:T(8,128)(2,1)} async-done(((bf16[64,256]{1,0:T(8,128)(2,1)}), bf16[2048,256]{1,0:T(8,128)(2,1)}) %all-gather.23.cloned.1.call-update) | async-done | bytes 1048592 | tf_op jit(solution)/shard_map/all_gather | solution.py:191
  767.0 4.2 fusion.27
  771.2 41.7 %all-reduce.5 = (f32[2048]{0:T(1024)S(1)}, f32[2048]{0:T(1024)S(1)}) all-reduce(f32[2048]{0:T(1024)S(1)} %get-tuple-element.46, f32[2048]{0:T(1024)S(1)} %copy-done.21), channel_id=5, replica_groups=mesh['dp'=4,'fsdp'=8] {'dp','fsdp'}, use_global_device_ids=true, to_apply=%region_12.13.clone | all-reduce | flops 4096 | bytes 32768
  814.0 3.5 fusion.26
  817.6 63.1 %reduce-scatter.14.cloned.1.call-done = bf16[176,2048]{1,0:T(8,128)(2,1)} async-done(((bf16[1408,2048]{1,0:T(8,128)(2,1)}), bf16[176,2048]{1,0:T(8,128)(2,1)}) %reduce-scatter.14.cloned.1.call-update) | async-done | bytes 720912 | tf_op jit(solution)/shard_map/reduce_scatter | solution.py:142
  880.6 2.4 convert_element_type.122
  883.0 357.3 %all-reduce.9.cloned.1.call-done = bf16[1408,2,2048]{2,1,0:T(2,128)(2,1)} async-done(((bf16[1408,2,2048]{2,1,0:T(2,128)(2,1)}), bf16[1408,2,2048]{2,1,0:T(2,128)(2,1)}) %all-reduce.9.cloned.1.call-update) | async-done | bytes 11534352
  1240.3 4.6 dynamic-slice_convert_fusion
  1244.9 207.6 %reduce-scatter.10.cloned.1.call-done = f32[64,2304]{1,0:T(8,128)} async-done(((f32[2048,2304]{1,0:T(8,128)}), f32[64,2304]{1,0:T(8,128)}) %reduce-scatter.10.cloned.1.call-update) | async-done | bytes 589840 | tf_op jit(solution)/shard_map/reduce_scatter | solution.py:201
  1452.5 1.9 slice.77
  1455.8 356.4 %reduce-scatter.12.cloned.1.call-done = f32[64,2048]{1,0:T(8,128)} async-done(((f32[2048,2048]{1,0:T(8,128)}), f32[64,2048]{1,0:T(8,128)}) %reduce-scatter.12.cloned.1.call-update) | async-done | bytes 524304 | tf_op jit(solution)/shard_map/reduce_scatter | solution.py:165
  (130 shorter events, 32.3 us)
Async XLA Ops:
  7.2 5.8 copy-start.27
  7.2 6.1 copy-start.28
  7.2 48.9 %copy-start.1 = (bf16[256,2048]{1,0:T(8,128)(2,1)S(1)}, bf16[256,2048]{1,0:T(8,128)(2,1)}, u32[]{:S(2)}) copy-start(bf16[256,2048]{1,0:T(8,128)(2,1)} %param.13) | copy-start | bytes 3145732
  7.2 89.4 %all-gather.9.cloned.1.call-start = ((), (), s32[]{:S(2)}) async-start(), calls=%async_computation.5 | async-start | bytes 9732096 | tf_op jit(solution)/shard_map/all_gather | solution.py:67
  9.1 166.6 %all-gather.11.cloned.1.call-start = ((), (), s32[]{:S(2)}) async-start(), calls=%async_computation.6 | async-start | bytes 8650752 | tf_op jit(solution)/shard_map/all_gather | solution.py:102
  9.8 330.9 %all-gather.15.cloned.1.call-start = ((), (), s32[]{:S(2)}) async-start(), calls=%async_computation.8 | async-start | bytes 12976128 | tf_op jit(solution)/shard_map/all_gather | solution.py:115
  12.9 362.5 %all-gather.13.cloned.1.call-start = ((), (), s32[]{:S(2)}) async-start(), calls=%async_computation.7 | async-start | bytes 5242880 | tf_op jit(solution)/shard_map/all_gather | solution.py:112
  56.0 48.7 %copy-start.23 = (f32[64]{0:T(128)}, f32[64]{0:T(128)S(1)}, u32[]{:S(2)}) copy-start(f32[64]{0:T(128)S(1)} %negate_power_fusion) | copy-start | bytes 772
  56.4 46.4 %copy-start.19 = (f32[256]{0:T(256)}, f32[256]{0:T(256)S(1)}, u32[]{:S(2)}) copy-start(f32[256]{0:T(256)S(1)} %add_rsqrt_fusion.1) | copy-start | bytes 3076
  104.7 1.0 copy-start.10
  105.7 3.1 copy-start.12
  105.7 3.1 copy-start.14
  108.8 1.4 copy-start.4
  108.8 1.5 copy-start.6
  110.3 2.0 copy-start
  110.3 3.9 copy-start.16
  110.3 2.0 copy-start.11
  112.3 1.9 copy-start.18
  181.8 2.0 copy-start.25
  181.8 2.0 copy-start.26
  181.9 5.8 copy-start.22
  183.1 228.8 %all-gather.19.cloned.1.call-start = ((), (), s32[]{:S(2)}) async-start(), calls=%async_computation.11 | async-start | bytes 5242880 | tf_op jit(solution)/shard_map/all_gather | solution.py:113
  187.7 318.9 %all-gather.17.cloned.1.call-start = ((), (), s32[]{:S(2)}) async-start(), calls=%async_computation.9 | async-start | bytes 6488064 | tf_op jit(solution)/shard_map/all_gather | solution.py:116
  188.3 428.5 %reduce-scatter.8.cloned.1.call-start = ((), (), s32[]{:S(2)}) async-start(), calls=%async_computation.12 | async-start | bytes 5242880 | tf_op jit(solution)/shard_map/reduce_scatter | solution.py:139
  522.3 1.6 copy-start.30
  522.3 2.5 copy-start.31
  541.1 90.1 %reduce-scatter.6.cloned.1.call-start = ((), (), s32[]{:S(2)}) async-start(), calls=%async_computation.10 | async-start | bytes 5242880 | tf_op jit(solution)/shard_map/reduce_scatter | solution.py:125
  552.3 159.3 %all-gather.21.cloned.1.call-start = ((), (), s32[]{:S(2)}) async-start(), calls=%async_computation.13 | async-start | bytes 8650752 | tf_op jit(solution)/shard_map/all_gather | solution.py:190
  553.0 214.0 %all-gather.23.cloned.1.call-start = ((), (), s32[]{:S(2)}) async-start(), calls=%async_computation.14 | async-start | bytes 1081344 | tf_op jit(solution)/shard_map/all_gather | solution.py:191
  553.6 327.0 %reduce-scatter.14.cloned.1.call-start = ((), (), s32[]{:S(2)}) async-start(), calls=%async_computation.17 | async-start | bytes 6488064 | tf_op jit(solution)/shard_map/reduce_scatter | solution.py:142
  564.2 676.1 %all-reduce.9.cloned.1.call-start = ((), (), s32[]{:S(2)}) async-start(), calls=%async_computation.18 | async-start | bytes 23068672
  612.0 0.9 copy-start.17
  612.1 840.4 %reduce-scatter.10.cloned.1.call-start = ((), (), s32[]{:S(2)}) async-start(), calls=%async_computation.15 | async-start | bytes 19464192 | tf_op jit(solution)/shard_map/reduce_scatter | solution.py:201
  615.3 31.7 %copy-start.8 = (f32[256,256]{0,1:T(8,128)}, f32[256,256]{0,1:T(8,128)S(1)}, u32[]{:S(2)}) copy-start(f32[256,256]{0,1:T(8,128)S(1)} %convert_multiply_fusion.5) | copy-start | bytes 786436
  635.7 1.3 copy-start.2
  643.3 3.7 copy-start.5
  647.0 9.3 copy-start.24
  670.3 3.1 copy-start.9
  673.3 12.8 copy-start.7
  673.3 4.1 copy-start.20
  686.1 1.6 copy-start.3
  686.2 1126.1 %reduce-scatter.12.cloned.1.call-start = ((), (), s32[]{:S(2)}) async-start(), calls=%async_computation.16 | async-start | bytes 17301504 | tf_op jit(solution)/shard_map/reduce_scatter | solution.py:165
  697.1 0.7 copy-start.29
  697.1 2.8 copy-start.13
  697.1 2.8 copy-start.15
  719.1 52.1 %copy-start.21 = (f32[2048]{0:T(1024)S(1)}, f32[2048]{0:T(1024)}, u32[]{:S(2)}) copy-start(f32[2048]{0:T(1024)} %get-tuple-element.44) | copy-start | bytes 24580
Sparse Core Ops, SparseCore 0:
  11.5 85.0 all-gather.8
  99.6 75.9 all-gather.10
  178.4 162.2 all-gather.14
  342.7 32.6 all-gather.12
  377.4 34.4 all-gather.18
  413.9 92.6 all-gather.16
  541.3 42.6 reduce-scatter.7
  586.7 44.5 reduce-scatter.5
  634.2 77.3 all-gather.20
  714.6 52.3 all-gather.22
  770.6 109.9 reduce-scatter.13
  884.4 355.8 all-reduce.8
  1246.7 205.7 reduce-scatter.9
  1455.2 357.0 reduce-scatter.11
